TPU v7x, 32 devices: a whole 2x2x4 slice. The times are simulated.
32 devices in a mesh: row: 8 (over y, x, core), col: 4 (over z).
Axes of the slice: x: 2, y: 2, z: 4, core: 2. Of those that a mesh axis runs over, the one named last changes fastest.
Arguments:
- resident_inverse: bfloat16 [24576, 24576], P('row', 'col')
- factor: bfloat16 [3, 24576, 512], P(None, 'row', 'col'), may hold values from -0.15625 to 0.15625
- diag_inverse: float32 [3, 512, 512], P(None, None, 'col'), may hold values from -4 to 4
- anc_tiles: int32 [3, 64], replicated, may hold values from -1 to 95, as said below
- slot_tile: int32 [96], replicated, may hold values from 0 to 95, as said below
Outputs:
- new_cols: bfloat16 [3, 24576, 512], P(None, 'row', 'col')
- diag_blocks: float32 [3, 512, 512], P(None, None, 'col')
Inputs may be any that keep to these rules, and one draw needn't show every extreme that they name: `anc_tiles`: row j lists the ancestor tiles of supernode j in ascending order, each at most once, followed by -1 in unused entries; every list holds tile 96 - 1; list 0 is full and list 2 has fewer than 32 tiles. A permutation of the tiles; slot s holds tile slot_tile[s], and each tile is stored within the same block of 24 consecutive slots as its own index. `resident_inverse` is symmetric. `resident_inverse` is symmetric.
All inputs are finite; a program needn't handle non-finite values.
Results may differ from a plain program's by a relative error of at most 0.017.
Values may be sent and summed in bfloat16 or wider, within the bound.
A program may use at most 128 MiB of HBM per device.

v0:
```python
import jax
import jax.numpy as jnp
from jax import lax
from jax.sharding import PartitionSpec as P


def broadcast(array, axis, root):
    mine = lax.axis_index(axis) == root
    return lax.psum(jnp.where(mine, array, jnp.zeros_like(array)), axis)


def slot_rows(anc_tiles, slot_tile, tile_rows):
    tile_count = slot_tile.shape[0]
    tile_ids = jnp.arange(tile_count, dtype=jnp.int32)
    listed = jnp.sum((anc_tiles[:, :, None] == tile_ids[None, None, :]).astype(jnp.float32), axis=1)
    onehot = (slot_tile[:, None] == tile_ids[None, :]).astype(jnp.float32)
    slot_mask = jnp.dot(listed, onehot.T, precision=lax.Precision.HIGHEST)
    return jnp.repeat(slot_mask, tile_rows, axis=1)


def on_device(resident_inverse, factor, diag_inverse, anc_tiles, slot_tile):
    own_rows = resident_inverse.shape[0]
    row_index = lax.axis_index("row")
    col_index = lax.axis_index("col")
    col_count = lax.axis_size("col")
    row_count = lax.axis_size("row")
    total_rows = own_rows * row_count
    row_mask = slot_rows(anc_tiles, slot_tile, total_rows // slot_tile.shape[0])
    own_mask = lax.dynamic_slice_in_dim(row_mask, row_index * own_rows, own_rows, 1)
    full_width = lax.all_gather(factor, "col", axis=2, tiled=True)
    masked_rows = full_width * own_mask.astype(jnp.bfloat16)[:, :, None]
    ratio = row_count // col_count
    pieces = []
    for within in range(ratio):
        pieces.append(broadcast(masked_rows, "row", col_index * ratio + within))
    masked_cols = jnp.concatenate(pieces, axis=1)
    partial_value = jnp.einsum(
        "rk,skw->srw", resident_inverse, masked_cols, preferred_element_type=jnp.float32
    )
    summed = lax.psum_scatter(
        partial_value.astype(jnp.bfloat16), "col", scatter_dimension=2, tiled=True
    ).astype(jnp.float32)
    new_cols = (-(summed * own_mask[:, :, None])).astype(jnp.bfloat16)
    contrib = jnp.einsum(
        "srw,srv->swv", masked_rows.astype(jnp.float32), summed, precision=lax.Precision.HIGHEST
    )
    totals = lax.psum(contrib.astype(jnp.bfloat16), "row").astype(jnp.float32)
    diag_blocks = diag_inverse + totals
    return (new_cols, diag_blocks)


def solution(mesh):
    placed = (P("row", "col"), P(None, "row", "col"), P(None, None, "col"), P(), P())
    return jax.shard_map(
        on_device,
        mesh=mesh,
        in_specs=placed,
        out_specs=(P(None, "row", "col"), P(None, None, "col")),
        check_vma=False,
    )
```

profile of v0, /device:TPU:0, one launch (start us, length us, event | category | flops | bytes accessed | tf_op | source)
XLA Modules:
  0.0 731.4 jit_solution(3939409600054093011)
XLA Ops:
  7.2 0.0 all-gather.2.cloned.1.call-start
  7.2 4.3 copy.10
  11.5 0.0 all-gather.2.cloned.1.call-update
  11.5 0.0 all-reduce.6.cloned.1.call-start
  11.6 0.8 convert_reduce_fusion
  12.4 0.9 fusion.15
  13.2 0.1 broadcast_bitcast_fusion
  13.4 0.2 copy.14
  13.6 0.6 fusion.18
  14.2 166.9 %all-gather.2.cloned.1.call-done = bf16[3,3072,512]{1,2,0:T(8,128)(2,1)} async-done(((bf16[3,3072,128]{1,2,0:T(8,128)(2,1)}), bf16[3,3072,512]{1,2,0:T(8,128)(2,1)}) %all-gather.2.cloned.1.call-update) | async-done | bytes 9437200 | tf_op jit(solution)/shard_map/all_gather | solution.py:30
  181.1 10.8 %broadcast_select_fusion.1 = (bf16[3,3072,512]{1,2,0:T(8,128)(2,1)}, bf16[3,3072,512]{1,2,0:T(8,128)(2,1)}) fusion(pred[]{:T(512)S(6)} %eq.32, bf16[3,3072,512]{1,2,0:T(8,128)(2,1)} %all-gather.2.cloned.1.call-done, bf16[3,3072]{1,0:T(4,128)(2,1)S(1)} %get-tuple-element.8, pred[]{:T(512)S(6)} %eq.39), kind=kLoop, calls=%fused_computation.7 | loop fusion | flops 14155776 | bytes 28329986 | tf_op jit(solution)/shard_map/jit(_where)/select_n | solution.py:9
  191.9 0.0 all-reduce.6.cloned.1.call-update
  191.9 0.0 reduce-scatter.2.cloned.1.call-start
  192.0 237.4 %all-reduce.6.cloned.1.call-done = (bf16[3,3072,512]{1,2,0:T(8,128)(2,1)}, bf16[3,3072,512]{1,2,0:T(8,128)(2,1)}) async-done(((bf16[3,3072,512]{1,2,0:T(8,128)(2,1)}, bf16[3,3072,512]{1,2,0:T(8,128)(2,1)}), (bf16[3,3072,512]{1,2,0:T(8,128)(2,1)}, bf16[3,3072,512]{1,2,0:T(8,128)(2,1)})) %all-reduce.6.cloned.1.call-update) | async-done | bytes 18874384 | tf_op jit(solution)/shard_map/psum | solution.py:9
  429.4 68.9 %convert_bitcast_fusion = bf16[3,3072,512]{1,2,0:T(8,128)(2,1)} fusion(bf16[3072,6144]{1,0:T(8,128)(2,1)} %param.5, bf16[3,3072,512]{1,2,0:T(8,128)(2,1)} %get-tuple-element.6, bf16[3,3072,512]{1,2,0:T(8,128)(2,1)} %get-tuple-element.7), kind=kOutput, calls=%fused_computation.5 | convolution fusion | flops 58024525824 | bytes 66060288 | tf_op jit(solution)/shard_map/rk,skw->srw/dot_general | solution.py:37
  498.3 0.0 reduce-scatter.2.cloned.1.call-update
  498.3 0.0 all-reduce.4.cloned.1.call-start
  498.3 161.4 %reduce-scatter.2.cloned.1.call-done = bf16[3,3072,128]{1,2,0:T(8,128)(2,1)} async-done(((bf16[3,3072,512]{1,2,0:T(8,128)(2,1)}), bf16[3,3072,128]{1,2,0:T(8,128)(2,1)}) %reduce-scatter.2.cloned.1.call-update) | async-done | bytes 2359312 | tf_op jit(solution)/shard_map/reduce_scatter | solution.py:40
  659.7 7.7 %fusion.12 = bf16[3,512,128]{2,1,0:T(8,128)(2,1)} fusion(bf16[3,3072,128]{1,2,0:T(8,128)(2,1)} %reduce-scatter.2.cloned.1.call-done, bf16[3,3072,512]{1,2,0:T(8,128)(2,1)} %all-gather.2.cloned.1.call-done, bf16[3,3072]{1,0:T(4,128)(2,1)S(1)} %get-tuple-element.8), kind=kOutput, calls=%fused_computation.12 | convolution fusion | flops 1212874752 | bytes 12208128 | tf_op jit(solution)/shard_map/srw,srv->swv/dot_general | solution.py:44
  667.4 0.0 all-reduce.4.cloned.1.call-update
  667.5 2.3 negate_convert_fusion
  669.8 2.4 copy.12
  672.2 50.7 %all-reduce.4.cloned.1.call-done = bf16[3,512,128]{2,1,0:T(8,128)(2,1)} async-done(((bf16[3,512,128]{2,1,0:T(8,128)(2,1)}), bf16[3,512,128]{2,1,0:T(8,128)(2,1)}) %all-reduce.4.cloned.1.call-update) | async-done | bytes 393232 | tf_op jit(solution)/shard_map/psum | solution.py:47
  722.9 1.9 convert_add_fusion
  (4 shorter events, 0.0 us)
Async XLA Ops:
  7.2 174.0 %all-gather.2.cloned.1.call-start = ((), (), s32[]{:S(2)}) async-start(), calls=%async_computation.1 | async-start | bytes 11796480 | tf_op jit(solution)/shard_map/all_gather | solution.py:30
  11.5 417.9 %all-reduce.6.cloned.1.call-start = ((), (), s32[]{:S(2)}) async-start(), calls=%async_computation.4 | async-start | bytes 37748736 | tf_op jit(solution)/shard_map/psum | solution.py:9
  191.9 467.8 %reduce-scatter.2.cloned.1.call-start = ((), (), s32[]{:S(2)}) async-start(), calls=%async_computation.2 | async-start | bytes 11796480 | tf_op jit(solution)/shard_map/reduce_scatter | solution.py:40
  498.3 169.2 %copy-start.1 = (f32[3,3072]{1,0:T(4,128)S(1)}, f32[3,3072]{1,0:T(4,128)}, u32[]{:S(2)}) copy-start(f32[3,3072]{1,0:T(4,128)} %get-tuple-element.9) | copy-start | bytes 110596
  498.3 224.6 %all-reduce.4.cloned.1.call-start = ((), (), s32[]{:S(2)}) async-start(), calls=%async_computation.3 | async-start | bytes 786432 | tf_op jit(solution)/shard_map/psum | solution.py:47
  667.4 55.5 %copy-start = (f32[3,512,128]{2,1,0:T(8,128)S(1)}, f32[3,512,128]{2,1,0:T(8,128)}, u32[]{:S(2)}) copy-start(f32[3,512,128]{2,1,0:T(8,128)} %param.7) | copy-start | bytes 2359300
Sparse Core Ops, SparseCore 0:
  11.6 169.4 all-gather.1
  192.0 237.2 all-reduce.5
  498.4 161.2 reduce-scatter.1
  667.6 55.3 all-reduce.3
where the time goes:
time: 732 us; the launch traced here: 731 us
  waiting for transfers between devices  617 us (84%)
  matrix products  77.5 us (11%)
  other arithmetic  16.4 us (2%)
  between operations  13.8 us (2%)
    psum x1, waiting for transfers between devices, broadcast(): return lax.psum(jnp.where(mine, array, jnp.zeros_like(array)), axis)  237 us
    all_gather x1, waiting for transfers between devices, on_device(): full_width = lax.all_gather(factor, 'col', axis=2, tiled=True)  167 us
    reduce_scatter x1, waiting for transfers between devices, on_device(): lax.psum_scatter(partial_value.astype(jnp.bfloat16), 'col', scatter_dimen...  161 us
    dot_general x1, matrix products, on_device(): jnp.einsum('rk,skw->srw', resident_inverse, masked_cols, preferred_elemen...  68.9 us
    psum x1, waiting for transfers between devices, on_device(): totals = lax.psum(contrib.astype(jnp.bfloat16), 'row').astype(jnp.float32)  50.7 us
  transfers between devices with their start and end apart: 4, of which 4 were waited for; matrix products, arithmetic and copies ran while one was open for 1% of the time, Pallas kernels for 0%

commit v1 on v0

v1 whole, which is shorter than its diff:
```python
import jax
import jax.numpy as jnp
from jax import lax
from jax.sharding import PartitionSpec as P


def slot_rows(anc_tiles, slot_tile, tile_rows):
    listed = (anc_tiles[:, :, None] == slot_tile[None, None, :]).any(axis=1)
    return jnp.repeat(listed.astype(jnp.float32), tile_rows, axis=1)


def on_device(resident_inverse, factor, diag_inverse, anc_tiles, slot_tile):
    own_rows = resident_inverse.shape[0]
    supers, _, part_width = factor.shape
    row_index = lax.axis_index("row")
    col_count = lax.axis_size("col")
    row_count = lax.axis_size("row")
    ratio = row_count // col_count
    total_rows = own_rows * row_count
    row_mask = slot_rows(anc_tiles, slot_tile, total_rows // slot_tile.shape[0])
    own_mask = lax.dynamic_slice_in_dim(row_mask, row_index * own_rows, own_rows, 1)
    mine = factor * own_mask.astype(jnp.bfloat16)[:, :, None]
    chunk = own_rows // row_count
    spread = mine.reshape(supers, row_count, chunk, part_width).transpose(1, 0, 2, 3)
    spread = lax.all_to_all(spread, "row", 0, 0, tiled=True)
    spread = spread.reshape(col_count, ratio * supers * chunk, part_width)
    spread = lax.all_to_all(spread, "col", 0, 0, tiled=True)
    spread = spread.reshape(col_count, ratio, supers, chunk, part_width)
    spread = spread.transpose(2, 1, 3, 0, 4).reshape(supers, ratio, chunk, col_count * part_width)
    spread, later = lax.optimization_barrier((spread, mine))
    col_index = lax.axis_index("col")

    last = col_count - 1
    up_moves = [(i, i + 1) for i in range(last)]
    down_moves = [(i + 1, i) for i in range(last)]

    def up(value):
        return lax.ppermute(value, "col", up_moves)

    def down(value):
        return lax.ppermute(value, "col", down_moves)

    gathered = [lax.all_gather(spread[s], "row", axis=1, tiled=True) for s in range(supers)]
    ups, downs = [later], [later]
    for by in range(last):
        low, high = ups[-1], downs[-1]
        if 0 < by <= supers:
            gathered[by - 1], low, high = lax.optimization_barrier((gathered[by - 1], low, high))
        ups.append(up(low))
        downs.append(down(high))
    partials = []
    for s in range(supers):
        blocks = gathered[s].reshape(ratio * own_rows, col_count * part_width)
        partials.append(
            jnp.dot(resident_inverse, blocks, preferred_element_type=jnp.float32).astype(jnp.bfloat16)
        )

    def piece(s, to):
        to = jnp.clip(to, 0, last) * part_width
        return lax.dynamic_slice_in_dim(partials[s], to, part_width, 1)

    kept = [piece(s, col_index) for s in range(supers)]
    kept[-1], ups, downs = lax.optimization_barrier((kept[-1], ups, downs))
    others = [later] + [ups[by] + downs[col_count - by] for by in range(1, col_count)]
    news, contribs = [], []
    for s in range(supers):
        from_below = piece(s, col_index + last)
        from_above = piece(s, col_index - last)
        for by in range(last, 0, -1):
            from_below, from_above = up(from_below), down(from_above)
            if by > 1:
                from_below = from_below + piece(s, col_index + by - 1)
                from_above = from_above + piece(s, col_index - by + 1)
        summed = (
            kept[s].astype(jnp.float32)
            + from_below.astype(jnp.float32)
            + from_above.astype(jnp.float32)
        )
        news.append((-(summed * own_mask[s][:, None])).astype(jnp.bfloat16))
        summed = summed.astype(jnp.bfloat16)
        contribs.append(jnp.stack([
            jnp.einsum("rw,rv->wv", other[s], summed, preferred_element_type=jnp.float32)
            for other in others
        ]))
    stacked = jnp.stack(contribs, axis=1)
    ordered = jnp.stack([
        lax.dynamic_index_in_dim(stacked, (col_index - q) % col_count, 0, keepdims=False)
        for q in range(col_count)
    ], axis=1)
    totals = ordered.reshape(supers, col_count * part_width, part_width)
    step = 1
    while step < row_count:
        sent = totals.astype(jnp.bfloat16)
        got = lax.ppermute(sent, "row", [(i, i ^ step) for i in range(row_count)])
        totals = sent.astype(jnp.float32) + got.astype(jnp.float32)
        step *= 2
    return (jnp.stack(news), diag_inverse + totals)


def solution(mesh):
    placed = (P("row", "col"), P(None, "row", "col"), P(None, None, "col"), P(), P())
    return jax.shard_map(
        on_device,
        mesh=mesh,
        in_specs=placed,
        out_specs=(P(None, "row", "col"), P(None, None, "col")),
        check_vma=False,
    )
```

time: 732 us -> 514 us (0.70)
  waiting for transfers between devices: 617 us -> 175 us
  blocking collectives: 0 us -> 92.4 us
  starting transfers between devices: 0.16 us -> 73.5 us
  local copies, waits for them, and re-layouts: 7.05 us -> 41.9 us
  other arithmetic: 16.4 us -> 24.3 us
    psum x2 -> x0, waiting for transfers between devices: 288 us -> none  [the longest x1 237 us: broadcast(): return lax.psum(jnp.where(mine, array, jnp.zeros_like(array)), axis)]
    ppermute x0 -> x27, waiting for transfers between devices: none -> 174 us  [the longest x12 91.3 us: up(): return lax.ppermute(value, 'col', up_moves)]
    all_gather x1 -> x3, waiting for transfers between devices: 167 us -> 0.04 us  [on_device(): lax.all_gather(spread[s], 'row', axis=1, tiled=True)]
    reduce_scatter x1 -> x0, waiting for transfers between devices: 161 us -> none  [on_device(): lax.psum_scatter(partial_value.astype(jnp.bfloat16), 'col', scatter_dimen...]
    all_to_all x0 -> x2, blocking collectives: none -> 92.4 us  [the longest x1 58 us: on_device(): spread = lax.all_to_all(spread, 'col', 0, 0, tiled=True)]
    ppermute x0 -> x27, starting transfers between devices: none -> 73.3 us  [the longest x12 54.5 us: up(): return lax.ppermute(value, 'col', up_moves)]
    optimization_barrier x0 -> x2, local copies, waits for them, and re-layouts: none -> 17.5 us  [on_device(): lax.optimization_barrier((gathered[by - 1], low, high))]
    add x1 -> x10, other arithmetic: 1.94 us -> 18.2 us  [the longest x6 8.66 us: on_device(): from_below = from_below + piece(s, col_index + by - 1)]
  transfers between devices with their start and end apart: 4 -> 30, of which waited for: 4 -> 17; matrix products, arithmetic and copies ran while one was open for 1% -> 27% of each run, Pallas kernels for 0% -> 0%
where the time goes in v1:
time: 514 us; the launch traced here: 506 us
  waiting for transfers between devices  175 us (34%)
  blocking collectives  92.4 us (18%)
  matrix products  84.8 us (16%)
  starting transfers between devices  73.5 us (14%)
  local copies, waits for them, and re-layouts  41.9 us (8%)
  other arithmetic  24.3 us (5%)
  between operations  14.7 us (3%)
    ppermute x12, waiting for transfers between devices, up(): return lax.ppermute(value, 'col', up_moves)  91.3 us
    dot_general x3, matrix products, on_device(): jnp.dot(resident_inverse, blocks, preferred_element_type=jnp.float32)  79.9 us
    ppermute x12, waiting for transfers between devices, down(): return lax.ppermute(value, 'col', down_moves)  64 us
    all_to_all x1, blocking collectives, on_device(): spread = lax.all_to_all(spread, 'col', 0, 0, tiled=True)  58 us
    ppermute x12, starting transfers between devices, up(): return lax.ppermute(value, 'col', up_moves)  54.5 us
    all_to_all x1, blocking collectives, on_device(): spread = lax.all_to_all(spread, 'row', 0, 0, tiled=True)  34.4 us
    ppermute x3, waiting for transfers between devices, on_device(): got = lax.ppermute(sent, 'row', [(i, i ^ step) for i in range(row_count)])  18.5 us
    optimization_barrier x2, local copies, waits for them, and re-layouts, on_device(): lax.optimization_barrier((gathered[by - 1], low, high))  17.5 us
  transfers between devices with their start and end apart: 30, of which 17 were waited for; matrix products, arithmetic and copies ran while one was open for 27% of the time, Pallas kernels for 0%

profile of v1, /device:TPU:0, one launch (start us, length us, event | category | flops | bytes accessed | tf_op | source)
XLA Modules:
  0.0 506.2 jit_solution(2496138775720817492)
XLA Ops:
  11.9 34.4 %all_to_all.10 = bf16[8,3,384,128]{3,2,1,0:T(8,128)(2,1)S(1)} all-to-all(bf16[8,3,384,128]{3,2,1,0:T(8,128)(2,1)S(1)} %copy.37), channel_id=1, replica_groups=mesh['row'=8,'col'=4] {'row'}, dimensions={0} | all-to-all | bytes 4718592 | tf_op jit(solution)/shard_map/all_to_all | solution.py:25
  46.2 58.0 %all_to_all.11 = bf16[4,2304,128]{2,1,0:T(8,128)(2,1)} all-to-all(bf16[4,2304,128]{2,1,0:T(8,128)(2,1)S(1)} %bitcast.191), channel_id=1, replica_groups=mesh['row'=8,'col'=4] {'col'}, dimensions={0} | all-to-all | bytes 4718592 | tf_op jit(solution)/shard_map/all_to_all | solution.py:27
  113.8 6.0 %collective-permute-start = (bf16[3,3072,128]{2,1,0:T(8,128)(2,1)S(1)}, bf16[3,3072,128]{2,1,0:T(8,128)(2,1)}, u32[]{:S(2)}, u32[]{:S(2)}) collective-permute-start(bf16[3,3072,128]{2,1,0:T(8,128)(2,1)S(1)} %broadcast_multiply_fusion), channel_id=1, source_target_pairs={{0,1},{1,2},{2,3},{4,5},{5,6},{6,7},{8,9},{9,10},{10,11},{12,13},{... | collective-permute-start | bytes 7077896 | tf_op jit(solution)/shard_map/ppermute | solution.py:38
  120.6 45.6 %collective-permute-done.1 = bf16[3,3072,128]{2,1,0:T(8,128)(2,1)} collective-permute-done((bf16[3,3072,128]{2,1,0:T(8,128)(2,1)S(1)}, bf16[3,3072,128]{2,1,0:T(8,128)(2,1)}, u32[]{:S(2)}, u32[]{:S(2)}) %collective-permute-start.1) | collective-permute-done | bytes 2359328 | tf_op jit(solution)/shard_map/ppermute | solution.py:41
  167.3 8.8 %copy.39 = bf16[2,3072,512]{2,1,0:T(8,128)(2,1)} copy(bf16[2,3072,512]{1,2,0:T(8,128)(2,1)} %bitcast.194) | data formatting | bytes 12582912 | tf_op jit(solution)/shard_map/optimization_barrier | solution.py:48
  176.0 25.9 %convolution_convert_fusion.2 = bf16[512,3072]{1,0:T(8,128)(2,1)S(1)} fusion(bf16[6144,512]{1,0:T(8,128)(2,1)} %bitcast.195, bf16[3072,6144]{1,0:T(8,128)(2,1)} %param.5), kind=kOutput, calls=%fused_computation.2 | convolution fusion | flops 19328925696 | bytes 47185920 | tf_op jit(solution)/shard_map/dot_general | solution.py:55
  203.3 5.4 %collective-permute-start.2 = (bf16[3072,128]{0,1:T(8,128)(2,1)}, bf16[3072,128]{0,1:T(8,128)(2,1)}, u32[]{:S(2)}, u32[]{:S(2)}) collective-permute-start(bf16[3072,128]{0,1:T(8,128)(2,1)} %get-tuple-element.50), channel_id=1, source_target_pairs={{0,1},{1,2},{2,3},{4,5},{5,6},{6,7},{8,9},{9,10},{10,11},{12,13},{... | collective-permute-start | bytes 2359304 | tf_op jit(solution)/shard_map/ppermute | solution.py:38
  210.0 6.0 %collective-permute-start.8 = (bf16[3,3072,128]{2,1,0:T(8,128)(2,1)}, bf16[3,3072,128]{2,1,0:T(8,128)(2,1)}, u32[]{:S(2)}, u32[]{:S(2)}) collective-permute-start(bf16[3,3072,128]{2,1,0:T(8,128)(2,1)} %collective-permute-done), channel_id=1, source_target_pairs={{0,1},{1,2},{2,3},{4,5},{5,6},{6,7},{8,9},{9,10},{10,11},{12,13},{... | collective-permute-start | bytes 7077896 | tf_op jit(solution)/shard_map/ppermute | solution.py:38
  217.6 8.7 %copy.41 = bf16[1,2,3072,512]{3,2,1,0:T(8,128)(2,1)} copy(bf16[1,2,3072,512]{2,3,1,0:T(8,128)(2,1)} %all-gather.11.cloned.1.call-done) | data formatting | bytes 12582912 | tf_op jit(solution)/shard_map/all_gather | solution.py:43
  226.2 28.2 %convolution_convert_fusion = bf16[512,3072]{1,0:T(8,128)(2,1)} fusion(bf16[6144,512]{1,0:T(8,128)(2,1)} %bitcast.196, bf16[3072,6144]{1,0:T(8,128)(2,1)} %param.5), kind=kOutput, calls=%fused_computation | convolution fusion | flops 19328925696 | bytes 47185920 | tf_op jit(solution)/shard_map/dot_general | solution.py:55
  258.8 6.3 %collective-permute-start.18 = (bf16[3072,128]{0,1:T(8,128)(2,1)}, bf16[3072,128]{0,1:T(8,128)(2,1)}, u32[]{:S(2)}, u32[]{:S(2)}) collective-permute-start(bf16[3072,128]{0,1:T(8,128)(2,1)} %get-tuple-element.60), channel_id=1, source_target_pairs={{0,1},{1,2},{2,3},{4,5},{5,6},{6,7},{8,9},{9,10},{10,11},{12,13},{... | collective-permute-start | bytes 2359304 | tf_op jit(solution)/shard_map/ppermute | solution.py:38
  272.2 4.4 collective-permute-done.8
  281.8 8.7 %copy.40 = bf16[2,3072,512]{2,1,0:T(8,128)(2,1)} copy(bf16[2,3072,512]{1,2,0:T(8,128)(2,1)} %bitcast.193) | data formatting | bytes 12582912 | tf_op jit(solution)/shard_map/optimization_barrier | solution.py:48
  290.6 25.9 %convolution_convert_fusion.1 = bf16[512,3072]{1,0:T(8,128)(2,1)S(1)} fusion(bf16[6144,512]{1,0:T(8,128)(2,1)} %bitcast.197, bf16[3072,6144]{1,0:T(8,128)(2,1)} %param.5), kind=kOutput, calls=%fused_computation.1 | convolution fusion | flops 19328925696 | bytes 47185920 | tf_op jit(solution)/shard_map/dot_general | solution.py:55
  322.1 4.6 collective-permute-start.19
  330.0 4.6 collective-permute-start.4
  345.8 7.5 %collective-permute-done.19 = bf16[3072,128]{0,1:T(8,128)(2,1)S(1)} collective-permute-done((bf16[3072,128]{0,1:T(8,128)(2,1)S(1)}, bf16[3072,128]{0,1:T(8,128)(2,1)S(1)}, u32[]{:S(2)}, u32[]{:S(2)}) %collective-permute-start.19) | collective-permute-done | bytes 786464 | tf_op jit(solution)/shard_map/ppermute | solution.py:38
  362.5 7.6 %collective-permute-done.4 = bf16[3072,128]{0,1:T(8,128)(2,1)S(1)} collective-permute-done((bf16[3072,128]{0,1:T(8,128)(2,1)S(1)}, bf16[3072,128]{0,1:T(8,128)(2,1)S(1)}, u32[]{:S(2)}, u32[]{:S(2)}) %collective-permute-start.4) | collective-permute-done | bytes 786464 | tf_op jit(solution)/shard_map/ppermute | solution.py:38
  370.2 4.4 collective-permute-start.20
  376.7 60.9 %collective-permute-done.11 = bf16[3072,128]{0,1:T(8,128)(2,1)S(1)} collective-permute-done((bf16[3072,128]{0,1:T(8,128)(2,1)S(1)}, bf16[3072,128]{0,1:T(8,128)(2,1)S(1)}, u32[]{:S(2)}, u32[]{:S(2)}) %collective-permute-start.11) | collective-permute-done | bytes 786464 | tf_op jit(solution)/shard_map/ppermute | solution.py:38
  446.5 7.9 %collective-permute-done.20 = bf16[3072,128]{0,1:T(8,128)(2,1)S(1)} collective-permute-done((bf16[3072,128]{0,1:T(8,128)(2,1)S(1)}, bf16[3072,128]{0,1:T(8,128)(2,1)S(1)}, u32[]{:S(2)}, u32[]{:S(2)}) %collective-permute-start.20) | collective-permute-done | bytes 786464 | tf_op jit(solution)/shard_map/ppermute | solution.py:38
  454.4 5.9 %collective-permute-done.23 = bf16[3072,128]{0,1:T(8,128)(2,1)S(1)} collective-permute-done((bf16[3072,128]{0,1:T(8,128)(2,1)S(1)}, bf16[3072,128]{0,1:T(8,128)(2,1)S(1)}, u32[]{:S(2)}, u32[]{:S(2)}) %collective-permute-start.23) | collective-permute-done | bytes 786464 | tf_op jit(solution)/shard_map/ppermute | solution.py:41
  477.3 9.7 %collective-permute-done.25 = bf16[3,512,128]{2,1,0:T(8,128)(2,1)S(1)} collective-permute-done((bf16[3,512,128]{2,1,0:T(8,128)(2,1)S(1)}, bf16[3,512,128]{2,1,0:T(8,128)(2,1)S(1)}, u32[]{:S(2)}, u32[]{:S(2)}) %collective-permute-start.25) | collective-permute-done | bytes 393248 | tf_op jit(solution)/shard_map/ppermute | solution.py:94
  490.4 7.1 %collective-permute-done.26 = bf16[3,512,128]{2,1,0:T(8,128)(2,1)} collective-permute-done((bf16[3,512,128]{2,1,0:T(8,128)(2,1)S(1)}, bf16[3,512,128]{2,1,0:T(8,128)(2,1)}, u32[]{:S(2)}, u32[]{:S(2)}) %collective-permute-start.26) | collective-permute-done | bytes 393248 | tf_op jit(solution)/shard_map/ppermute | solution.py:94
  (113 shorter events, 99.1 us)
Async XLA Ops:
  7.2 160.1 %all-gather.7.cloned.1.call-start = ((), (), s32[]{:S(2)}) async-start(), calls=%async_computation.2 | async-start | bytes 7077888 | tf_op jit(solution)/shard_map/all_gather | solution.py:43
  111.7 105.9 %all-gather.11.cloned.1.call-start = ((), (), s32[]{:S(2)}) async-start(), calls=%async_computation.4 | async-start | bytes 7077888 | tf_op jit(solution)/shard_map/all_gather | solution.py:43
  112.4 165.9 %all-gather.9.cloned.1.call-start = ((), (), s32[]{:S(2)}) async-start(), calls=%async_computation.3 | async-start | bytes 7077888 | tf_op jit(solution)/shard_map/all_gather | solution.py:43
  112.5 53.7 %collective-permute-start.1 = (bf16[3,3072,128]{2,1,0:T(8,128)(2,1)S(1)}, bf16[3,3072,128]{2,1,0:T(8,128)(2,1)}, u32[]{:S(2)}, u32[]{:S(2)}) collective-permute-start(bf16[3,3072,128]{2,1,0:T(8,128)(2,1)S(1)} %broadcast_multiply_fusion), channel_id=1, source_target_pairs={{1,0},{2,1},{3,2},{5,4},{6,5},{7,6},{9,8},{10,9},{11,10},{13,12},{... | collective-permute-start | bytes 7077896 | tf_op jit(solution)/shard_map/ppermute | solution.py:41
  113.8 53.5 %collective-permute-start = (bf16[3,3072,128]{2,1,0:T(8,128)(2,1)S(1)}, bf16[3,3072,128]{2,1,0:T(8,128)(2,1)}, u32[]{:S(2)}, u32[]{:S(2)}) collective-permute-start(bf16[3,3072,128]{2,1,0:T(8,128)(2,1)S(1)} %broadcast_multiply_fusion), channel_id=1, source_target_pairs={{0,1},{1,2},{2,3},{4,5},{5,6},{6,7},{8,9},{9,10},{10,11},{12,13},{... | collective-permute-start | bytes 7077896 | tf_op jit(solution)/shard_map/ppermute | solution.py:38
  203.3 55.5 %collective-permute-start.2 = (bf16[3072,128]{0,1:T(8,128)(2,1)}, bf16[3072,128]{0,1:T(8,128)(2,1)}, u32[]{:S(2)}, u32[]{:S(2)}) collective-permute-start(bf16[3072,128]{0,1:T(8,128)(2,1)} %get-tuple-element.50), channel_id=1, source_target_pairs={{0,1},{1,2},{2,3},{4,5},{5,6},{6,7},{8,9},{9,10},{10,11},{12,13},{... | collective-permute-start | bytes 2359304 | tf_op jit(solution)/shard_map/ppermute | solution.py:38
  208.7 56.5 %collective-permute-start.5 = (bf16[3072,128]{0,1:T(8,128)(2,1)}, bf16[3072,128]{0,1:T(8,128)(2,1)}, u32[]{:S(2)}, u32[]{:S(2)}) collective-permute-start(bf16[3072,128]{0,1:T(8,128)(2,1)} %get-tuple-element.51), channel_id=1, source_target_pairs={{1,0},{2,1},{3,2},{5,4},{6,5},{7,6},{9,8},{10,9},{11,10},{13,12},{... | collective-permute-start | bytes 2359304 | tf_op jit(solution)/shard_map/ppermute | solution.py:41
  210.0 66.6 %collective-permute-start.8 = (bf16[3,3072,128]{2,1,0:T(8,128)(2,1)}, bf16[3,3072,128]{2,1,0:T(8,128)(2,1)}, u32[]{:S(2)}, u32[]{:S(2)}) collective-permute-start(bf16[3,3072,128]{2,1,0:T(8,128)(2,1)} %collective-permute-done), channel_id=1, source_target_pairs={{0,1},{1,2},{2,3},{4,5},{5,6},{6,7},{8,9},{9,10},{10,11},{12,13},{... | collective-permute-start | bytes 7077896 | tf_op jit(solution)/shard_map/ppermute | solution.py:38
  216.0 65.8 %collective-permute-start.9 = (bf16[3,3072,128]{2,1,0:T(8,128)(2,1)}, bf16[3,3072,128]{2,1,0:T(8,128)(2,1)}, u32[]{:S(2)}, u32[]{:S(2)}) collective-permute-start(bf16[3,3072,128]{2,1,0:T(8,128)(2,1)} %collective-permute-done.1), channel_id=1, source_target_pairs={{1,0},{2,1},{3,2},{5,4},{6,5},{7,6},{9,8},{10,9},{11,10},{13,12},{... | collective-permute-start | bytes 7077896 | tf_op jit(solution)/shard_map/ppermute | solution.py:41
  257.5 61.1 %collective-permute-start.21 = (bf16[3072,128]{0,1:T(8,128)(2,1)}, bf16[3072,128]{0,1:T(8,128)(2,1)}, u32[]{:S(2)}, u32[]{:S(2)}) collective-permute-start(bf16[3072,128]{0,1:T(8,128)(2,1)} %get-tuple-element.59), channel_id=1, source_target_pairs={{1,0},{2,1},{3,2},{5,4},{6,5},{7,6},{9,8},{10,9},{11,10},{13,12},{... | collective-permute-start | bytes 2359304 | tf_op jit(solution)/shard_map/ppermute | solution.py:41
  258.8 61.4 %collective-permute-start.18 = (bf16[3072,128]{0,1:T(8,128)(2,1)}, bf16[3072,128]{0,1:T(8,128)(2,1)}, u32[]{:S(2)}, u32[]{:S(2)}) collective-permute-start(bf16[3072,128]{0,1:T(8,128)(2,1)} %get-tuple-element.60), channel_id=1, source_target_pairs={{0,1},{1,2},{2,3},{4,5},{5,6},{6,7},{8,9},{9,10},{10,11},{12,13},{... | collective-permute-start | bytes 2359304 | tf_op jit(solution)/shard_map/ppermute | solution.py:38
  268.2 58.5 %collective-permute-start.3 = (bf16[3072,128]{0,1:T(8,128)(2,1)}, bf16[3072,128]{0,1:T(8,128)(2,1)}, u32[]{:S(2)}, u32[]{:S(2)}) collective-permute-start(bf16[3072,128]{0,1:T(8,128)(2,1)} %get-tuple-element.48), channel_id=1, source_target_pairs={{0,1},{1,2},{2,3},{4,5},{5,6},{6,7},{8,9},{9,10},{10,11},{12,13},{... | collective-permute-start | bytes 2359304 | tf_op jit(solution)/shard_map/ppermute | solution.py:38
  276.5 51.5 %collective-permute-start.6 = (bf16[3072,128]{0,1:T(8,128)(2,1)}, bf16[3072,128]{0,1:T(8,128)(2,1)}, u32[]{:S(2)}, u32[]{:S(2)}) collective-permute-start(bf16[3072,128]{0,1:T(8,128)(2,1)} %get-tuple-element.49), channel_id=1, source_target_pairs={{1,0},{2,1},{3,2},{5,4},{6,5},{7,6},{9,8},{10,9},{11,10},{13,12},{... | collective-permute-start | bytes 2359304 | tf_op jit(solution)/shard_map/ppermute | solution.py:41
  322.1 31.2 %collective-permute-start.19 = (bf16[3072,128]{0,1:T(8,128)(2,1)S(1)}, bf16[3072,128]{0,1:T(8,128)(2,1)S(1)}, u32[]{:S(2)}, u32[]{:S(2)}) collective-permute-start(bf16[3072,128]{0,1:T(8,128)(2,1)S(1)} %get-tuple-element.63), channel_id=1, source_target_pairs={{0,1},{1,2},{2,3},{4,5},{5,6},{6,7},{8,9},{9,10},{10,11},{12,13},{... | collective-permute-start | bytes 2359304 | tf_op jit(solution)/shard_map/ppermute | solution.py:38
  326.7 31.3 %collective-permute-start.22 = (bf16[3072,128]{0,1:T(8,128)(2,1)S(1)}, bf16[3072,128]{0,1:T(8,128)(2,1)S(1)}, u32[]{:S(2)}, u32[]{:S(2)}) collective-permute-start(bf16[3072,128]{0,1:T(8,128)(2,1)S(1)} %get-tuple-element.64), channel_id=1, source_target_pairs={{1,0},{2,1},{3,2},{5,4},{6,5},{7,6},{9,8},{10,9},{11,10},{13,12},{... | collective-permute-start | bytes 2359304 | tf_op jit(solution)/shard_map/ppermute | solution.py:41
  330.0 40.2 %collective-permute-start.4 = (bf16[3072,128]{0,1:T(8,128)(2,1)S(1)}, bf16[3072,128]{0,1:T(8,128)(2,1)S(1)}, u32[]{:S(2)}, u32[]{:S(2)}) collective-permute-start(bf16[3072,128]{0,1:T(8,128)(2,1)S(1)} %get-tuple-element.46), channel_id=1, source_target_pairs={{0,1},{1,2},{2,3},{4,5},{5,6},{6,7},{8,9},{9,10},{10,11},{12,13},{... | collective-permute-start | bytes 2359304 | tf_op jit(solution)/shard_map/ppermute | solution.py:38
  336.5 38.4 %collective-permute-start.7 = (bf16[3072,128]{0,1:T(8,128)(2,1)S(1)}, bf16[3072,128]{0,1:T(8,128)(2,1)S(1)}, u32[]{:S(2)}, u32[]{:S(2)}) collective-permute-start(bf16[3072,128]{0,1:T(8,128)(2,1)S(1)} %get-tuple-element.47), channel_id=1, source_target_pairs={{1,0},{2,1},{3,2},{5,4},{6,5},{7,6},{9,8},{10,9},{11,10},{13,12},{... | collective-permute-start | bytes 2359304 | tf_op jit(solution)/shard_map/ppermute | solution.py:41
  341.2 103.8 %collective-permute-start.16 = (bf16[3,3072,128]{2,1,0:T(8,128)(2,1)}, bf16[3,3072,128]{2,1,0:T(8,128)(2,1)S(1)}, u32[]{:S(2)}, u32[]{:S(2)}) collective-permute-start(bf16[3,3072,128]{2,1,0:T(8,128)(2,1)} %collective-permute-done.8), channel_id=1, source_target_pairs={{0,1},{1,2},{2,3},{4,5},{5,6},{6,7},{8,9},{9,10},{10,11},{12,13},{... | collective-permute-start | bytes 7077896 | tf_op jit(solution)/shard_map/ppermute | solution.py:38
  353.3 93.2 %collective-permute-start.17 = (bf16[3,3072,128]{2,1,0:T(8,128)(2,1)}, bf16[3,3072,128]{2,1,0:T(8,128)(2,1)S(1)}, u32[]{:S(2)}, u32[]{:S(2)}) collective-permute-start(bf16[3,3072,128]{2,1,0:T(8,128)(2,1)} %collective-permute-done.9), channel_id=1, source_target_pairs={{1,0},{2,1},{3,2},{5,4},{6,5},{7,6},{9,8},{10,9},{11,10},{13,12},{... | collective-permute-start | bytes 7077896 | tf_op jit(solution)/shard_map/ppermute | solution.py:41
  358.0 79.5 %collective-permute-start.11 = (bf16[3072,128]{0,1:T(8,128)(2,1)S(1)}, bf16[3072,128]{0,1:T(8,128)(2,1)S(1)}, u32[]{:S(2)}, u32[]{:S(2)}) collective-permute-start(bf16[3072,128]{0,1:T(8,128)(2,1)S(1)} %get-tuple-element.54), channel_id=1, source_target_pairs={{0,1},{1,2},{2,3},{4,5},{5,6},{6,7},{8,9},{9,10},{10,11},{12,13},{... | collective-permute-start | bytes 2359304 | tf_op jit(solution)/shard_map/ppermute | solution.py:38
  370.2 84.3 %collective-permute-start.20 = (bf16[3072,128]{0,1:T(8,128)(2,1)S(1)}, bf16[3072,128]{0,1:T(8,128)(2,1)S(1)}, u32[]{:S(2)}, u32[]{:S(2)}) collective-permute-start(bf16[3072,128]{0,1:T(8,128)(2,1)S(1)} %get-tuple-element.61), channel_id=1, source_target_pairs={{0,1},{1,2},{2,3},{4,5},{5,6},{6,7},{8,9},{9,10},{10,11},{12,13},{... | collective-permute-start | bytes 2359304 | tf_op jit(solution)/shard_map/ppermute | solution.py:38
  374.9 66.2 %collective-permute-start.14 = (bf16[3072,128]{0,1:T(8,128)(2,1)S(1)}, bf16[3072,128]{0,1:T(8,128)(2,1)S(1)}, u32[]{:S(2)}, u32[]{:S(2)}) collective-permute-start(bf16[3072,128]{0,1:T(8,128)(2,1)S(1)} %get-tuple-element.55), channel_id=1, source_target_pairs={{1,0},{2,1},{3,2},{5,4},{6,5},{7,6},{9,8},{10,9},{11,10},{13,12},{... | collective-permute-start | bytes 2359304 | tf_op jit(solution)/shard_map/ppermute | solution.py:41
  441.7 29.6 %collective-permute-start.12 = (bf16[3072,128]{0,1:T(8,128)(2,1)S(1)}, bf16[3072,128]{0,1:T(8,128)(2,1)S(1)}, u32[]{:S(2)}, u32[]{:S(2)}) collective-permute-start(bf16[3072,128]{0,1:T(8,128)(2,1)S(1)} %get-tuple-element.52), channel_id=1, source_target_pairs={{0,1},{1,2},{2,3},{4,5},{5,6},{6,7},{8,9},{9,10},{10,11},{12,13},{... | collective-permute-start | bytes 2359304 | tf_op jit(solution)/shard_map/ppermute | solution.py:38
  445.0 26.4 %collective-permute-start.15 = (bf16[3072,128]{0,1:T(8,128)(2,1)S(1)}, bf16[3072,128]{0,1:T(8,128)(2,1)S(1)}, u32[]{:S(2)}, u32[]{:S(2)}) collective-permute-start(bf16[3072,128]{0,1:T(8,128)(2,1)S(1)} %get-tuple-element.53), channel_id=1, source_target_pairs={{1,0},{2,1},{3,2},{5,4},{6,5},{7,6},{9,8},{10,9},{11,10},{13,12},{... | collective-permute-start | bytes 2359304 | tf_op jit(solution)/shard_map/ppermute | solution.py:41
  (15 other events, 396.5 us)
Sparse Core Ops, SparseCore 0:
  111.8 44.5 all-gather.6
  158.2 46.5 all-gather.10
  207.3 46.5 all-gather.8
